TPU v7x, 32 devices: a whole 2x2x4 slice. The times are simulated.
32 devices in a mesh: shots: 2 (over y), wide: 16 (over z, x, core).
Axes of the slice: x: 2, y: 2, z: 4, core: 2. Of those that a mesh axis runs over, the one named last changes fastest.
Arguments:
- src_now: float32 [32, 64, 128], P('wide', 'shots'), parts along dimension 1, may hold values from -6 to 6
- src_old: float32 [32, 64, 128], P('wide', 'shots'), parts along dimension 1, may hold values from -6 to 6
- rcv_now: float32 [32, 256, 32], P('wide', 'shots'), parts along dimension 1, may hold values from -6 to 6
- rcv_old: float32 [32, 256, 32], P('wide', 'shots'), parts along dimension 1, may hold values from -6 to 6
- medium: float32 [3, 32, 128, 32], P(None, 'wide'), may hold values from 0.04 to 0.24
- wavelet: float32 [4], replicated, may hold values from -4 to 4
- shot: int32 [6], P('shots'), parts along dimension 0, may hold values from 0 to 31
- traces: float32 [32, 128, 4], P('wide', 'shots'), parts along dimension 1, may hold values from -6 to 6
- rec_x: int32 [32, 128], P('wide', 'shots'), parts along dimension 1, may hold values from 0 to 31
- lag_order: int32 [33], replicated, may hold values from 0 to 32, each once
Outputs:
- src_next: float32 [32, 64, 128], P('wide', 'shots'), parts along dimension 1
- src_prior: float32 [32, 64, 128], P('wide', 'shots'), parts along dimension 1
- rcv_next: float32 [32, 256, 32], P('wide', 'shots'), parts along dimension 1
- rcv_prior: float32 [32, 256, 32], P('wide', 'shots'), parts along dimension 1
- image: float32 [66, 32, 128, 32], P('shots', 'wide'), parts along dimension 0
There are 2 independent parts, one for each index of `shots`. A program takes and returns all parts, laid end to end along the dimension named above; an argument that names none is the same for every part. Nothing has to cross between parts.
Inputs may be any that keep to these rules, and one draw needn't show every extreme that they name: `lag_order`: each of the 33 lag slots once.
All inputs are finite; a program needn't handle non-finite values.
Results may differ from a plain program's by a relative error of at most 0.0003.
Values sent between devices are 32-bit elements; how exact they have to be, the bound alone decides.
A program may use at most 64 MiB of HBM per device.

v0:
```python
import jax
import jax.numpy as jnp
from jax import lax
from jax.sharding import PartitionSpec as P


def extended(array, sides, width):
    for axis, dim in sides:
        devices, length = (lax.axis_size(axis), array.shape[dim])
        up = [(i, (i + 1) % devices) for i in range(devices - 1)]
        down = [(j, i) for i, j in up]
        last = lax.slice_in_dim(array, length - width, length, axis=dim)
        initial = lax.slice_in_dim(array, 0, width, axis=dim)
        before = lax.ppermute(last, axis, up)
        after = lax.ppermute(initial, axis, down)
        array = jnp.concatenate([before, array, after], axis=dim)
    return array


def window_sum(padded, dim, count):

    def window_at(start):
        return lax.slice_in_dim(padded, start, start + count, axis=dim)

    return (
        -1.0 / 12.0 * (window_at(0) + window_at(4))
        + 4.0 / 3.0 * (window_at(1) + window_at(3))
        - 2.5 * window_at(2)
    )


def widen(field, dim):
    widths = [(0, 0)] * field.ndim
    widths[dim] = (2, 2)
    return jnp.pad(field, widths)


def second(field, dim):
    return window_sum(widen(field, dim), dim, field.shape[dim])


def lagged(snaps, lag_order):
    half = (lag_order.shape[0] - 1) // 2
    cells_x = snaps[0][0].shape[2]
    widths = ((0, 0), (0, 0), (half, half))
    padded = [(jnp.pad(source, widths), jnp.pad(receiver, widths)) for source, receiver in snaps]

    def one_plane(slot):
        offset = slot - half
        total = None
        for source, receiver in padded:
            moved_src = lax.dynamic_slice_in_dim(source, half - offset, cells_x, 2)
            moved_rcv = lax.dynamic_slice_in_dim(receiver, half + offset, cells_x, 2)
            product = moved_src * moved_rcv
            total = product if total is None else total + product
        return total

    return lax.map(one_plane, lag_order)


def indicator(count, first, target):
    return (jnp.arange(count, dtype=jnp.int32) + first == target).astype(jnp.float32)


def on_device(src_now, src_old, rcv_now, rcv_old, medium, wavelet, shot, traces, rec_x, lag_order):
    slab_x, cells_y, cells_z = src_now.shape
    slab_y, _, cells_x = rcv_now.shape
    device = lax.axis_index("wide")
    steps = wavelet.shape[0]
    onehot = (rec_x[:, :, None] == jnp.arange(cells_x, dtype=jnp.int32)[None, None, :]).astype(
        jnp.float32
    )
    shot_rcv = (
        indicator(slab_y, device * slab_y, shot[1])[:, None, None]
        * indicator(cells_z, 0, shot[2])[None, :, None]
        * indicator(cells_x, 0, shot[0])[None, None, :]
    )
    snaps = []
    turned_now, turned_old = (
        lax.all_to_all(src_now, "wide", split_axis=1, concat_axis=0, tiled=True),
        lax.all_to_all(src_old, "wide", split_axis=1, concat_axis=0, tiled=True),
    )
    pair_now = jnp.stack([jnp.transpose(turned_now, (1, 2, 0)), rcv_now])
    pair_old = jnp.stack([jnp.transpose(turned_old, (1, 2, 0)), rcv_old])
    for step in range(steps):
        widened = extended(pair_now, (("wide", 1),), 2)
        spread = (
            medium[0] * second(pair_now, 3)
            + medium[1] * window_sum(widened, 1, slab_y)
            + medium[2] * second(pair_now, 2)
        )
        pair_new = 2.0 * pair_now - pair_old + spread
        pair_new = pair_new.at[0].add(-wavelet[step] * shot_rcv)
        pair_new = pair_new.at[1, :, 0, :].add(
            jnp.einsum("yr,yrx->yx", traces[:, :, step], onehot, precision=lax.Precision.HIGHEST)
        )
        pair_old, pair_now = (pair_now, pair_new)
        if step % 2 == 1:
            snaps.append((pair_now[0], pair_now[1]))
    back_now, back_old = (
        lax.all_to_all(pair_now[0], "wide", split_axis=2, concat_axis=0, tiled=True),
        lax.all_to_all(pair_old[0], "wide", split_axis=2, concat_axis=0, tiled=True),
    )
    src_next = jnp.transpose(back_now, (2, 0, 1))
    src_prior = jnp.transpose(back_old, (2, 0, 1))
    return (src_next, src_prior, pair_now[1], pair_old[1], lagged(snaps, lag_order))


def solution(mesh):
    return jax.shard_map(
        on_device,
        mesh=mesh,
        in_specs=(
            P("wide", "shots", None),
            P("wide", "shots", None),
            P("wide", "shots", None),
            P("wide", "shots", None),
            P(None, "wide", None, None),
            P(),
            P("shots"),
            P("wide", "shots", None),
            P("wide", "shots"),
            P(),
        ),
        out_specs=(
            P("wide", "shots", None),
            P("wide", "shots", None),
            P("wide", "shots", None),
            P("wide", "shots", None),
            P("shots", "wide", None, None),
        ),
        check_vma=False,
    )
```

profile of v0, /device:TPU:0, one launch (start us, length us, event | category | flops | bytes accessed | tf_op | source)
XLA Modules:
  0.0 220.2 jit_solution(10086139652803222354)
XLA Ops:
  0.7 1.4 copy.55
  2.1 7.4 %all-to-all-start = ((f32[2,32,128]{2,0,1:T(2,128)}), f32[2,32,128]{2,0,1:T(2,128)S(1)}, u32[]{:S(2)}, u32[]{:S(2)}) async-start(f32[2,32,128]{2,0,1:T(2,128)} %copy.55), calls=%async_computation | async-start | bytes 65536 | tf_op jit(solution)/shard_map/all_to_all | solution.py:80
  9.5 0.8 slice_bitcast_fusion.8
  10.3 1.4 copy.57
  11.7 1.4 fusion.109
  13.0 0.6 compare_convert_fusion.1
  13.7 0.7 compare_convert_fusion.2
  14.4 1.4 fusion.108
  16.5 6.0 %all-to-all-start.1 = ((f32[2,32,128]{2,0,1:T(2,128)}), f32[2,32,128]{2,0,1:T(2,128)S(1)}, u32[]{:S(2)}, u32[]{:S(2)}) async-start(f32[2,32,128]{2,0,1:T(2,128)} %copy.57), calls=%async_computation.1 | async-start | bytes 65536 | tf_op jit(solution)/shard_map/all_to_all | solution.py:81
  22.5 0.8 pad_maximum_fusion.10
  23.3 2.3 %collective-permute-start = (f32[2,2,128,32]{2,3,1,0:T(8,128)S(1)}, f32[2,2,128,32]{2,3,1,0:T(8,128)S(1)}, u32[]{:S(2)}, u32[]{:S(2)}) collective-permute-start(f32[2,2,128,32]{2,3,1,0:T(8,128)S(1)} %pad_maximum_fusion.10), channel_id=1, source_target_pairs={{0,1},{1,2},{2,3},{3,4},{4,5},{5,6},{6,7},{7,8},{8,9},{9,10},{10,1... | collective-permute-start | bytes 196616 | tf_op jit(solution)/shard_map/ppermute | solution.py:14
  25.6 1.3 collective-permute-start.1
  26.9 0.7 compare_convert_fusion
  27.5 1.6 all-to-all-done.1
  29.1 0.7 collective-permute-done.1
  29.9 0.9 fusion.11
  31.3 4.8 %collective-permute-start.2 = (f32[2,2,128,32]{2,3,1,0:T(8,128)S(1)}, f32[2,2,128,32]{2,3,1,0:T(8,128)S(1)}, u32[]{:S(2)}, u32[]{:S(2)}) collective-permute-start(f32[2,2,128,32]{2,3,1,0:T(8,128)S(1)} %scatter-add.29), channel_id=1, source_target_pairs={{0,1},{1,2},{2,3},{3,4},{4,5},{5,6},{6,7},{7,8},{8,9},{9,10},{10,1... | collective-permute-start | bytes 196616 | tf_op jit(solution)/shard_map/ppermute | solution.py:14
  36.2 1.3 collective-permute-start.3
  38.1 1.2 collective-permute-done.3
  40.0 5.1 %collective-permute-start.4 = (f32[2,2,128,32]{2,3,1,0:T(8,128)S(1)}, f32[2,2,128,32]{2,3,1,0:T(8,128)S(1)}, u32[]{:S(2)}, u32[]{:S(2)}) collective-permute-start(f32[2,2,128,32]{2,3,1,0:T(8,128)S(1)} %scatter-add.31), channel_id=1, source_target_pairs={{0,1},{1,2},{2,3},{3,4},{4,5},{5,6},{6,7},{7,8},{8,9},{9,10},{10,1... | collective-permute-start | bytes 196616 | tf_op jit(solution)/shard_map/ppermute | solution.py:14
  45.1 1.3 collective-permute-start.5
  48.9 5.3 %collective-permute-start.6 = (f32[2,2,128,32]{2,3,1,0:T(8,128)S(1)}, f32[2,2,128,32]{2,3,1,0:T(8,128)S(1)}, u32[]{:S(2)}, u32[]{:S(2)}) collective-permute-start(f32[2,2,128,32]{2,3,1,0:T(8,128)S(1)} %scatter-add.35), channel_id=1, source_target_pairs={{0,1},{1,2},{2,3},{3,4},{4,5},{5,6},{6,7},{7,8},{8,9},{9,10},{10,1... | collective-permute-start | bytes 196616 | tf_op jit(solution)/shard_map/ppermute | solution.py:14
  54.1 1.3 collective-permute-start.7
  56.1 0.6 copy.66
  56.7 7.4 %all-to-all-start.3 = ((f32[2,128,32]{1,0,2:T(2,128)}), f32[2,128,32]{1,0,2:T(2,128)S(1)}, u32[]{:S(2)}, u32[]{:S(2)}) async-start(f32[2,128,32]{1,0,2:T(2,128)} %copy.66), calls=%async_computation.3 | async-start | bytes 65536 | tf_op jit(solution)/shard_map/all_to_all | solution.py:102
  64.2 6.6 %all-to-all-done.3 = f32[2,128,32]{1,0,2:T(2,128)S(1)} async-done(((f32[2,128,32]{1,0,2:T(2,128)}), f32[2,128,32]{1,0,2:T(2,128)S(1)}, u32[]{:S(2)}, u32[]{:S(2)}) %all-to-all-start.3) | async-done | bytes 32800 | tf_op jit(solution)/shard_map/all_to_all | solution.py:102
  70.8 0.6 copy.68
  72.1 0.6 copy.63
  72.8 3.5 %all-to-all-start.2 = ((f32[2,128,32]{1,0,2:T(2,128)}), f32[2,128,32]{1,0,2:T(2,128)S(1)}, u32[]{:S(2)}, u32[]{:S(2)}) async-start(f32[2,128,32]{1,0,2:T(2,128)} %copy.63), calls=%async_computation.2 | async-start | bytes 65536 | tf_op jit(solution)/shard_map/all_to_all | solution.py:101
  76.3 143.2 %while.23 = (s32[]{:T(128)}, f32[33,2,128,32]{2,3,1,0:T(8,128)}, s32[33]{0:T(128)S(1)}, f32[2,128,64]{1,2,0:T(8,128)S(1)}, f32[2,128,64]{1,2,0:T(8,128)S(1)}, /*...) while((s32[]{:T(128)}, f32[33,2,128,32]{2,3,1,0:T(8,128)}, ...), condition=%wide.region_1.2_spmd, body=%wide.region_0.1_spmd.sunk | while | flops 24586 | bytes 819957 | solution.py:58
  80.0 0.6 constant_dynamic-update-slice_fusion.2
  84.3 0.6 constant_dynamic-update-slice_fusion.2
  88.7 0.6 constant_dynamic-update-slice_fusion.2
  93.0 0.6 constant_dynamic-update-slice_fusion.2
  97.4 0.6 constant_dynamic-update-slice_fusion.2
  101.7 0.6 constant_dynamic-update-slice_fusion.2
  106.0 0.6 constant_dynamic-update-slice_fusion.2
  110.4 0.6 constant_dynamic-update-slice_fusion.2
  114.7 0.6 constant_dynamic-update-slice_fusion.2
  123.4 0.6 constant_dynamic-update-slice_fusion.2
  127.7 0.6 constant_dynamic-update-slice_fusion.2
  136.4 0.6 constant_dynamic-update-slice_fusion.2
  140.8 0.6 constant_dynamic-update-slice_fusion.2
  145.1 0.6 constant_dynamic-update-slice_fusion.2
  149.4 0.6 constant_dynamic-update-slice_fusion.2
  153.8 0.6 constant_dynamic-update-slice_fusion.2
  158.1 0.6 constant_dynamic-update-slice_fusion.2
  219.5 0.6 copy.65
  (359 shorter events, 51.2 us)
Async XLA Ops:
  0.6 38.7 %copy-start = (f32[2,128,32]{1,2,0:T(8,128)S(1)}, f32[2,128,32]{1,2,0:T(8,128)}, u32[]{:S(2)}) copy-start(f32[2,128,32]{1,2,0:T(8,128)} %param.30) | copy-start | bytes 98308
  0.6 30.2 %copy-start.2 = (f32[2,64,4]{1,2,0:T(4,128)S(1)}, f32[2,64,4]{1,2,0:T(4,128)}, u32[]{:S(2)}) copy-start(f32[2,64,4]{1,2,0:T(4,128)} %param.35) | copy-start | bytes 6148
  0.7 30.2 %copy-start.3 = (s32[2,64]{1,0:T(2,128)S(1)}, s32[2,64]{1,0:T(2,128)}, u32[]{:S(2)}) copy-start(s32[2,64]{1,0:T(2,128)} %param.36) | copy-start | bytes 1540
  2.1 14.4 %all-to-all-start = ((f32[2,32,128]{2,0,1:T(2,128)}), f32[2,32,128]{2,0,1:T(2,128)S(1)}, u32[]{:S(2)}, u32[]{:S(2)}) async-start(f32[2,32,128]{2,0,1:T(2,128)} %copy.55), calls=%async_computation | async-start | bytes 65536 | tf_op jit(solution)/shard_map/all_to_all | solution.py:80
  16.5 12.7 %all-to-all-start.1 = ((f32[2,32,128]{2,0,1:T(2,128)}), f32[2,32,128]{2,0,1:T(2,128)S(1)}, u32[]{:S(2)}, u32[]{:S(2)}) async-start(f32[2,32,128]{2,0,1:T(2,128)} %copy.57), calls=%async_computation.1 | async-start | bytes 65536 | tf_op jit(solution)/shard_map/all_to_all | solution.py:81
  23.3 5.9 %collective-permute-start = (f32[2,2,128,32]{2,3,1,0:T(8,128)S(1)}, f32[2,2,128,32]{2,3,1,0:T(8,128)S(1)}, u32[]{:S(2)}, u32[]{:S(2)}) collective-permute-start(f32[2,2,128,32]{2,3,1,0:T(8,128)S(1)} %pad_maximum_fusion.10), channel_id=1, source_target_pairs={{0,1},{1,2},{2,3},{3,4},{4,5},{5,6},{6,7},{7,8},{8,9},{9,10},{10,1... | collective-permute-start | bytes 196616 | tf_op jit(solution)/shard_map/ppermute | solution.py:14
  25.6 4.3 %collective-permute-start.1 = (f32[2,2,128,32]{2,3,1,0:T(8,128)S(1)}, f32[2,2,128,32]{2,3,1,0:T(8,128)S(1)}, u32[]{:S(2)}, u32[]{:S(2)}) collective-permute-start(f32[2,2,128,32]{2,3,1,0:T(8,128)S(1)} %pad_maximum_fusion.10), channel_id=1, source_target_pairs={{1,0},{2,1},{3,2},{4,3},{5,4},{6,5},{7,6},{8,7},{9,8},{10,9},{11,1... | collective-permute-start | bytes 196616 | tf_op jit(solution)/shard_map/ppermute | solution.py:15
  31.3 6.8 %collective-permute-start.2 = (f32[2,2,128,32]{2,3,1,0:T(8,128)S(1)}, f32[2,2,128,32]{2,3,1,0:T(8,128)S(1)}, u32[]{:S(2)}, u32[]{:S(2)}) collective-permute-start(f32[2,2,128,32]{2,3,1,0:T(8,128)S(1)} %scatter-add.29), channel_id=1, source_target_pairs={{0,1},{1,2},{2,3},{3,4},{4,5},{5,6},{6,7},{7,8},{8,9},{9,10},{10,1... | collective-permute-start | bytes 196616 | tf_op jit(solution)/shard_map/ppermute | solution.py:14
  36.2 3.1 %collective-permute-start.3 = (f32[2,2,128,32]{2,3,1,0:T(8,128)S(1)}, f32[2,2,128,32]{2,3,1,0:T(8,128)S(1)}, u32[]{:S(2)}, u32[]{:S(2)}) collective-permute-start(f32[2,2,128,32]{2,3,1,0:T(8,128)S(1)} %scatter-add.29), channel_id=1, source_target_pairs={{1,0},{2,1},{3,2},{4,3},{5,4},{6,5},{7,6},{8,7},{9,8},{10,9},{11,1... | collective-permute-start | bytes 196616 | tf_op jit(solution)/shard_map/ppermute | solution.py:15
  40.0 7.7 %collective-permute-start.4 = (f32[2,2,128,32]{2,3,1,0:T(8,128)S(1)}, f32[2,2,128,32]{2,3,1,0:T(8,128)S(1)}, u32[]{:S(2)}, u32[]{:S(2)}) collective-permute-start(f32[2,2,128,32]{2,3,1,0:T(8,128)S(1)} %scatter-add.31), channel_id=1, source_target_pairs={{0,1},{1,2},{2,3},{3,4},{4,5},{5,6},{6,7},{7,8},{8,9},{9,10},{10,1... | collective-permute-start | bytes 196616 | tf_op jit(solution)/shard_map/ppermute | solution.py:14
  45.1 3.1 %collective-permute-start.5 = (f32[2,2,128,32]{2,3,1,0:T(8,128)S(1)}, f32[2,2,128,32]{2,3,1,0:T(8,128)S(1)}, u32[]{:S(2)}, u32[]{:S(2)}) collective-permute-start(f32[2,2,128,32]{2,3,1,0:T(8,128)S(1)} %scatter-add.31), channel_id=1, source_target_pairs={{1,0},{2,1},{3,2},{4,3},{5,4},{6,5},{7,6},{8,7},{9,8},{10,9},{11,1... | collective-permute-start | bytes 196616 | tf_op jit(solution)/shard_map/ppermute | solution.py:15
  48.4 27.9 %copy-start.4 = (s32[33]{0:T(128)S(1)}, s32[33]{0:T(128)}, u32[]{:S(2)}) copy-start(s32[33]{0:T(128)} %param.37) | copy-start | bytes 400
  48.9 22.5 %collective-permute-start.6 = (f32[2,2,128,32]{2,3,1,0:T(8,128)S(1)}, f32[2,2,128,32]{2,3,1,0:T(8,128)S(1)}, u32[]{:S(2)}, u32[]{:S(2)}) collective-permute-start(f32[2,2,128,32]{2,3,1,0:T(8,128)S(1)} %scatter-add.35), channel_id=1, source_target_pairs={{0,1},{1,2},{2,3},{3,4},{4,5},{5,6},{6,7},{7,8},{8,9},{9,10},{10,1... | collective-permute-start | bytes 196616 | tf_op jit(solution)/shard_map/ppermute | solution.py:14
  54.1 17.3 %collective-permute-start.7 = (f32[2,2,128,32]{2,3,1,0:T(8,128)S(1)}, f32[2,2,128,32]{2,3,1,0:T(8,128)S(1)}, u32[]{:S(2)}, u32[]{:S(2)}) collective-permute-start(f32[2,2,128,32]{2,3,1,0:T(8,128)S(1)} %scatter-add.35), channel_id=1, source_target_pairs={{1,0},{2,1},{3,2},{4,3},{5,4},{6,5},{7,6},{8,7},{9,8},{10,9},{11,1... | collective-permute-start | bytes 196616 | tf_op jit(solution)/shard_map/ppermute | solution.py:15
  56.7 14.0 %all-to-all-start.3 = ((f32[2,128,32]{1,0,2:T(2,128)}), f32[2,128,32]{1,0,2:T(2,128)S(1)}, u32[]{:S(2)}, u32[]{:S(2)}) async-start(f32[2,128,32]{1,0,2:T(2,128)} %copy.66), calls=%async_computation.3 | async-start | bytes 65536 | tf_op jit(solution)/shard_map/all_to_all | solution.py:102
  72.1 4.2 %copy-start.1 = (f32[2,128,32]{1,2,0:T(8,128)}, f32[2,128,32]{1,2,0:T(8,128)S(1)}, u32[]{:S(2)}) copy-start(f32[2,128,32]{1,2,0:T(8,128)S(1)} %get-tuple-element.340) | copy-start | bytes 98308
  72.8 146.7 %all-to-all-start.2 = ((f32[2,128,32]{1,0,2:T(2,128)}), f32[2,128,32]{1,0,2:T(2,128)S(1)}, u32[]{:S(2)}, u32[]{:S(2)}) async-start(f32[2,128,32]{1,0,2:T(2,128)} %copy.63), calls=%async_computation.2 | async-start | bytes 65536 | tf_op jit(solution)/shard_map/all_to_all | solution.py:101
where the time goes:
time: 224 us; the launch traced here: 220 us
  loops' own time  85 us (38%)
  local copies, waits for them, and re-layouts  67.3 us (30%)
  starting transfers between devices  47 us (21%)
  waiting for transfers between devices  10.6 us (5%)
  other arithmetic  5.48 us (2%)
  between operations  3.54 us (2%)
    another operation x1, loops' own time, lagged(): return lax.map(one_plane, lag_order)  85 us
    dynamic_update_slice x66, local copies, waits for them, and re-layouts, lagged(): return lax.map(one_plane, lag_order)  23 us
    dynamic_slice x33, local copies, waits for them, and re-layouts, lagged(): return lax.map(one_plane, lag_order)  19.9 us
    ppermute x4, starting transfers between devices, extended(): before = lax.ppermute(last, axis, up)  17.5 us
    dynamic_slice x132, local copies, waits for them, and re-layouts, one_plane(): moved_rcv = lax.dynamic_slice_in_dim(receiver, half + offset, cells_x, 2)  7.68 us
    all_to_all x1, starting transfers between devices, on_device(): lax.all_to_all(pair_old[0], 'wide', split_axis=2, concat_axis=0, tiled=True)  7.41 us
    all_to_all x1, starting transfers between devices, on_device(): lax.all_to_all(src_now, 'wide', split_axis=1, concat_axis=0, tiled=True)  7.39 us
    all_to_all x1, waiting for transfers between devices, on_device(): lax.all_to_all(pair_old[0], 'wide', split_axis=2, concat_axis=0, tiled=True)  6.59 us
  transfers between devices with their start and end apart: 12, of which 5 were waited for; matrix products, arithmetic and copies ran while one was open for 31% of the time, Pallas kernels for 0%

commit v1 on v0

--- a/solution.py
+++ b/solution.py
@@ -99,7 +99,12 @@
             snaps.append((pair_now[0], pair_now[1]))
     back_now, back_old = (
         lax.all_to_all(pair_now[0], "wide", split_axis=2, concat_axis=0, tiled=True),
-        lax.all_to_all(pair_old[0], "wide", split_axis=2, concat_axis=0, tiled=True),
+        jnp.concatenate(
+            lax.all_to_all(
+                jnp.stack(jnp.split(pair_old[0], lax.axis_size("wide"), axis=2)), "wide", 0, 0
+            ),
+            axis=0,
+        ),
     )
     src_next = jnp.transpose(back_now, (2, 0, 1))
     src_prior = jnp.transpose(back_old, (2, 0, 1))

time: 224 us -> 233 us (1.040)
  local copies, waits for them, and re-layouts: 67.3 us -> 76 us
    unnamed x12 -> x27, local copies, waits for them, and re-layouts: 2.84 us -> 11.5 us
  transfers between devices with their start and end apart: 12 -> 12, of which waited for: 5 -> 5; matrix products, arithmetic and copies ran while one was open for 31% -> 33% of each run, Pallas kernels for 0% -> 0%
where the time goes in v1:
time: 233 us; the launch traced here: 229 us
  loops' own time  85 us (36%)
  local copies, waits for them, and re-layouts  76 us (33%)
  starting transfers between devices  47 us (20%)
  waiting for transfers between devices  10.6 us (5%)
  other arithmetic  5.48 us (2%)
  between operations  3.55 us (2%)
    another operation x1, loops' own time, lagged(): return lax.map(one_plane, lag_order)  85 us
    dynamic_update_slice x66, local copies, waits for them, and re-layouts, lagged(): return lax.map(one_plane, lag_order)  23 us
    dynamic_slice x33, local copies, waits for them, and re-layouts, lagged(): return lax.map(one_plane, lag_order)  19.9 us
    ppermute x4, starting transfers between devices, extended(): before = lax.ppermute(last, axis, up)  17.5 us
    unnamed x27, local copies, waits for them, and re-layouts  11.5 us
    dynamic_slice x132, local copies, waits for them, and re-layouts, one_plane(): moved_rcv = lax.dynamic_slice_in_dim(receiver, half + offset, cells_x, 2)  7.68 us
    all_to_all x1, starting transfers between devices, on_device(): lax.all_to_all(jnp.stack(jnp.split(pair_old[0], lax.axis_size('wide'), ax...  7.41 us
    all_to_all x1, starting transfers between devices, on_device(): lax.all_to_all(src_now, 'wide', split_axis=1, concat_axis=0, tiled=True)  7.39 us
  transfers between devices with their start and end apart: 12, of which 5 were waited for; matrix products, arithmetic and copies ran while one was open for 33% of the time, Pallas kernels for 0%

profile of v1, /device:TPU:0, one launch (start us, length us, event | category | flops | bytes accessed | tf_op | source)
XLA Modules:
  0.0 228.8 jit_solution(15906311758644785957)
XLA Ops:
  0.7 1.4 copy.55
  2.1 7.4 %all-to-all-start = ((f32[2,32,128]{2,0,1:T(2,128)}), f32[2,32,128]{2,0,1:T(2,128)S(1)}, u32[]{:S(2)}, u32[]{:S(2)}) async-start(f32[2,32,128]{2,0,1:T(2,128)} %copy.55), calls=%async_computation | async-start | bytes 65536 | tf_op jit(solution)/shard_map/all_to_all | solution.py:80
  9.5 0.8 slice_bitcast_fusion.8
  10.3 1.4 copy.57
  11.7 1.4 fusion.109
  13.0 0.6 compare_convert_fusion.1
  13.7 0.7 compare_convert_fusion.2
  14.4 1.4 fusion.108
  16.5 6.0 %all-to-all-start.1 = ((f32[2,32,128]{2,0,1:T(2,128)}), f32[2,32,128]{2,0,1:T(2,128)S(1)}, u32[]{:S(2)}, u32[]{:S(2)}) async-start(f32[2,32,128]{2,0,1:T(2,128)} %copy.57), calls=%async_computation.1 | async-start | bytes 65536 | tf_op jit(solution)/shard_map/all_to_all | solution.py:81
  22.5 0.8 pad_maximum_fusion.10
  23.3 2.3 %collective-permute-start = (f32[2,2,128,32]{2,3,1,0:T(8,128)S(1)}, f32[2,2,128,32]{2,3,1,0:T(8,128)S(1)}, u32[]{:S(2)}, u32[]{:S(2)}) collective-permute-start(f32[2,2,128,32]{2,3,1,0:T(8,128)S(1)} %pad_maximum_fusion.10), channel_id=1, source_target_pairs={{0,1},{1,2},{2,3},{3,4},{4,5},{5,6},{6,7},{7,8},{8,9},{9,10},{10,1... | collective-permute-start | bytes 196616 | tf_op jit(solution)/shard_map/ppermute | solution.py:14
  25.6 1.3 collective-permute-start.1
  26.9 0.7 compare_convert_fusion
  27.5 1.6 all-to-all-done.1
  29.1 0.7 collective-permute-done.1
  29.9 0.9 fusion.11
  31.3 4.8 %collective-permute-start.2 = (f32[2,2,128,32]{2,3,1,0:T(8,128)S(1)}, f32[2,2,128,32]{2,3,1,0:T(8,128)S(1)}, u32[]{:S(2)}, u32[]{:S(2)}) collective-permute-start(f32[2,2,128,32]{2,3,1,0:T(8,128)S(1)} %scatter-add.29), channel_id=1, source_target_pairs={{0,1},{1,2},{2,3},{3,4},{4,5},{5,6},{6,7},{7,8},{8,9},{9,10},{10,1... | collective-permute-start | bytes 196616 | tf_op jit(solution)/shard_map/ppermute | solution.py:14
  36.2 1.3 collective-permute-start.3
  38.1 1.2 collective-permute-done.3
  40.0 5.1 %collective-permute-start.4 = (f32[2,2,128,32]{2,3,1,0:T(8,128)S(1)}, f32[2,2,128,32]{2,3,1,0:T(8,128)S(1)}, u32[]{:S(2)}, u32[]{:S(2)}) collective-permute-start(f32[2,2,128,32]{2,3,1,0:T(8,128)S(1)} %scatter-add.31), channel_id=1, source_target_pairs={{0,1},{1,2},{2,3},{3,4},{4,5},{5,6},{6,7},{7,8},{8,9},{9,10},{10,1... | collective-permute-start | bytes 196616 | tf_op jit(solution)/shard_map/ppermute | solution.py:14
  45.1 1.3 collective-permute-start.5
  48.9 5.3 %collective-permute-start.6 = (f32[2,2,128,32]{2,3,1,0:T(8,128)S(1)}, f32[2,2,128,32]{2,3,1,0:T(8,128)S(1)}, u32[]{:S(2)}, u32[]{:S(2)}) collective-permute-start(f32[2,2,128,32]{2,3,1,0:T(8,128)S(1)} %scatter-add.35), channel_id=1, source_target_pairs={{0,1},{1,2},{2,3},{3,4},{4,5},{5,6},{6,7},{7,8},{8,9},{9,10},{10,1... | collective-permute-start | bytes 196616 | tf_op jit(solution)/shard_map/ppermute | solution.py:14
  54.1 1.3 collective-permute-start.7
  65.4 7.4 %all-to-all-start.3 = ((f32[16,2,128,2]{2,3,1,0:T(2,128)}), f32[16,2,128,2]{2,3,1,0:T(2,128)S(1)}, u32[]{:S(2)}, u32[]{:S(2)}) async-start(f32[16,2,128,2]{2,3,1,0:T(2,128)} %constant_dynamic-update-slice_fusion.1), calls=%async_computation.3 | async-start | bytes 65536 | tf_op jit(solution)/shard_map/all_to_all | solution.py:103
  72.8 6.6 %all-to-all-done.3 = f32[16,2,128,2]{2,3,1,0:T(2,128)S(1)} async-done(((f32[16,2,128,2]{2,3,1,0:T(2,128)}), f32[16,2,128,2]{2,3,1,0:T(2,128)S(1)}, u32[]{:S(2)}, u32[]{:S(2)}) %all-to-all-start.3) | async-done | bytes 32800 | tf_op jit(solution)/shard_map/all_to_all | solution.py:103
  80.7 0.6 copy.63
  81.4 3.5 %all-to-all-start.2 = ((f32[2,128,32]{1,0,2:T(2,128)}), f32[2,128,32]{1,0,2:T(2,128)S(1)}, u32[]{:S(2)}, u32[]{:S(2)}) async-start(f32[2,128,32]{1,0,2:T(2,128)} %copy.63), calls=%async_computation.2 | async-start | bytes 65536 | tf_op jit(solution)/shard_map/all_to_all | solution.py:101
  84.9 143.2 %while.23 = (s32[]{:T(128)}, f32[33,2,128,32]{2,3,1,0:T(8,128)}, s32[33]{0:T(128)S(1)}, f32[2,128,64]{1,2,0:T(8,128)S(1)}, f32[2,128,64]{1,2,0:T(8,128)S(1)}, /*...) while((s32[]{:T(128)}, f32[33,2,128,32]{2,3,1,0:T(8,128)}, ...), condition=%wide.region_1.2_spmd, body=%wide.region_0.1_spmd.sunk | while | flops 24586 | bytes 819957 | solution.py:58
  93.0 0.6 constant_dynamic-update-slice_fusion.18
  97.3 0.6 constant_dynamic-update-slice_fusion.18
  106.0 0.6 constant_dynamic-update-slice_fusion.18
  110.3 0.6 constant_dynamic-update-slice_fusion.18
  114.7 0.6 constant_dynamic-update-slice_fusion.18
  119.0 0.6 constant_dynamic-update-slice_fusion.18
  123.4 0.6 constant_dynamic-update-slice_fusion.18
  127.7 0.6 constant_dynamic-update-slice_fusion.18
  132.0 0.6 constant_dynamic-update-slice_fusion.18
  136.4 0.6 constant_dynamic-update-slice_fusion.18
  140.7 0.6 constant_dynamic-update-slice_fusion.18
  145.1 0.6 constant_dynamic-update-slice_fusion.18
  149.4 0.6 constant_dynamic-update-slice_fusion.18
  153.7 0.6 constant_dynamic-update-slice_fusion.18
  158.1 0.6 constant_dynamic-update-slice_fusion.18
  162.4 0.6 constant_dynamic-update-slice_fusion.18
  166.7 0.6 constant_dynamic-update-slice_fusion.18
  175.4 0.6 constant_dynamic-update-slice_fusion.18
  179.8 0.6 constant_dynamic-update-slice_fusion.18
  228.1 0.6 copy.65
  (373 shorter events, 59.8 us)
Async XLA Ops:
  0.6 38.7 %copy-start = (f32[2,128,32]{1,2,0:T(8,128)S(1)}, f32[2,128,32]{1,2,0:T(8,128)}, u32[]{:S(2)}) copy-start(f32[2,128,32]{1,2,0:T(8,128)} %param.30) | copy-start | bytes 98308
  0.6 30.2 %copy-start.2 = (f32[2,64,4]{1,2,0:T(4,128)S(1)}, f32[2,64,4]{1,2,0:T(4,128)}, u32[]{:S(2)}) copy-start(f32[2,64,4]{1,2,0:T(4,128)} %param.35) | copy-start | bytes 6148
  0.7 30.2 %copy-start.3 = (s32[2,64]{1,0:T(2,128)S(1)}, s32[2,64]{1,0:T(2,128)}, u32[]{:S(2)}) copy-start(s32[2,64]{1,0:T(2,128)} %param.36) | copy-start | bytes 1540
  2.1 14.4 %all-to-all-start = ((f32[2,32,128]{2,0,1:T(2,128)}), f32[2,32,128]{2,0,1:T(2,128)S(1)}, u32[]{:S(2)}, u32[]{:S(2)}) async-start(f32[2,32,128]{2,0,1:T(2,128)} %copy.55), calls=%async_computation | async-start | bytes 65536 | tf_op jit(solution)/shard_map/all_to_all | solution.py:80
  16.5 12.7 %all-to-all-start.1 = ((f32[2,32,128]{2,0,1:T(2,128)}), f32[2,32,128]{2,0,1:T(2,128)S(1)}, u32[]{:S(2)}, u32[]{:S(2)}) async-start(f32[2,32,128]{2,0,1:T(2,128)} %copy.57), calls=%async_computation.1 | async-start | bytes 65536 | tf_op jit(solution)/shard_map/all_to_all | solution.py:81
  23.3 5.9 %collective-permute-start = (f32[2,2,128,32]{2,3,1,0:T(8,128)S(1)}, f32[2,2,128,32]{2,3,1,0:T(8,128)S(1)}, u32[]{:S(2)}, u32[]{:S(2)}) collective-permute-start(f32[2,2,128,32]{2,3,1,0:T(8,128)S(1)} %pad_maximum_fusion.10), channel_id=1, source_target_pairs={{0,1},{1,2},{2,3},{3,4},{4,5},{5,6},{6,7},{7,8},{8,9},{9,10},{10,1... | collective-permute-start | bytes 196616 | tf_op jit(solution)/shard_map/ppermute | solution.py:14
  25.6 4.3 %collective-permute-start.1 = (f32[2,2,128,32]{2,3,1,0:T(8,128)S(1)}, f32[2,2,128,32]{2,3,1,0:T(8,128)S(1)}, u32[]{:S(2)}, u32[]{:S(2)}) collective-permute-start(f32[2,2,128,32]{2,3,1,0:T(8,128)S(1)} %pad_maximum_fusion.10), channel_id=1, source_target_pairs={{1,0},{2,1},{3,2},{4,3},{5,4},{6,5},{7,6},{8,7},{9,8},{10,9},{11,1... | collective-permute-start | bytes 196616 | tf_op jit(solution)/shard_map/ppermute | solution.py:15
  31.3 6.8 %collective-permute-start.2 = (f32[2,2,128,32]{2,3,1,0:T(8,128)S(1)}, f32[2,2,128,32]{2,3,1,0:T(8,128)S(1)}, u32[]{:S(2)}, u32[]{:S(2)}) collective-permute-start(f32[2,2,128,32]{2,3,1,0:T(8,128)S(1)} %scatter-add.29), channel_id=1, source_target_pairs={{0,1},{1,2},{2,3},{3,4},{4,5},{5,6},{6,7},{7,8},{8,9},{9,10},{10,1... | collective-permute-start | bytes 196616 | tf_op jit(solution)/shard_map/ppermute | solution.py:14
  36.2 3.1 %collective-permute-start.3 = (f32[2,2,128,32]{2,3,1,0:T(8,128)S(1)}, f32[2,2,128,32]{2,3,1,0:T(8,128)S(1)}, u32[]{:S(2)}, u32[]{:S(2)}) collective-permute-start(f32[2,2,128,32]{2,3,1,0:T(8,128)S(1)} %scatter-add.29), channel_id=1, source_target_pairs={{1,0},{2,1},{3,2},{4,3},{5,4},{6,5},{7,6},{8,7},{9,8},{10,9},{11,1... | collective-permute-start | bytes 196616 | tf_op jit(solution)/shard_map/ppermute | solution.py:15
  40.0 7.7 %collective-permute-start.4 = (f32[2,2,128,32]{2,3,1,0:T(8,128)S(1)}, f32[2,2,128,32]{2,3,1,0:T(8,128)S(1)}, u32[]{:S(2)}, u32[]{:S(2)}) collective-permute-start(f32[2,2,128,32]{2,3,1,0:T(8,128)S(1)} %scatter-add.31), channel_id=1, source_target_pairs={{0,1},{1,2},{2,3},{3,4},{4,5},{5,6},{6,7},{7,8},{8,9},{9,10},{10,1... | collective-permute-start | bytes 196616 | tf_op jit(solution)/shard_map/ppermute | solution.py:14
  45.1 3.1 %collective-permute-start.5 = (f32[2,2,128,32]{2,3,1,0:T(8,128)S(1)}, f32[2,2,128,32]{2,3,1,0:T(8,128)S(1)}, u32[]{:S(2)}, u32[]{:S(2)}) collective-permute-start(f32[2,2,128,32]{2,3,1,0:T(8,128)S(1)} %scatter-add.31), channel_id=1, source_target_pairs={{1,0},{2,1},{3,2},{4,3},{5,4},{6,5},{7,6},{8,7},{9,8},{10,9},{11,1... | collective-permute-start | bytes 196616 | tf_op jit(solution)/shard_map/ppermute | solution.py:15
  48.4 36.5 %copy-start.4 = (s32[33]{0:T(128)S(1)}, s32[33]{0:T(128)}, u32[]{:S(2)}) copy-start(s32[33]{0:T(128)} %param.37) | copy-start | bytes 400
  48.9 31.2 %collective-permute-start.6 = (f32[2,2,128,32]{2,3,1,0:T(8,128)S(1)}, f32[2,2,128,32]{2,3,1,0:T(8,128)S(1)}, u32[]{:S(2)}, u32[]{:S(2)}) collective-permute-start(f32[2,2,128,32]{2,3,1,0:T(8,128)S(1)} %scatter-add.35), channel_id=1, source_target_pairs={{0,1},{1,2},{2,3},{3,4},{4,5},{5,6},{6,7},{7,8},{8,9},{9,10},{10,1... | collective-permute-start | bytes 196616 | tf_op jit(solution)/shard_map/ppermute | solution.py:14
  54.1 25.9 %collective-permute-start.7 = (f32[2,2,128,32]{2,3,1,0:T(8,128)S(1)}, f32[2,2,128,32]{2,3,1,0:T(8,128)S(1)}, u32[]{:S(2)}, u32[]{:S(2)}) collective-permute-start(f32[2,2,128,32]{2,3,1,0:T(8,128)S(1)} %scatter-add.35), channel_id=1, source_target_pairs={{1,0},{2,1},{3,2},{4,3},{5,4},{6,5},{7,6},{8,7},{9,8},{10,9},{11,1... | collective-permute-start | bytes 196616 | tf_op jit(solution)/shard_map/ppermute | solution.py:15
  65.4 14.0 %all-to-all-start.3 = ((f32[16,2,128,2]{2,3,1,0:T(2,128)}), f32[16,2,128,2]{2,3,1,0:T(2,128)S(1)}, u32[]{:S(2)}, u32[]{:S(2)}) async-start(f32[16,2,128,2]{2,3,1,0:T(2,128)} %constant_dynamic-update-slice_fusion.1), calls=%async_computation.3 | async-start | bytes 65536 | tf_op jit(solution)/shard_map/all_to_all | solution.py:103
  80.7 4.2 %copy-start.1 = (f32[2,128,32]{1,2,0:T(8,128)}, f32[2,128,32]{1,2,0:T(8,128)S(1)}, u32[]{:S(2)}) copy-start(f32[2,128,32]{1,2,0:T(8,128)S(1)} %get-tuple-element.340) | copy-start | bytes 98308
  81.4 146.7 %all-to-all-start.2 = ((f32[2,128,32]{1,0,2:T(2,128)}), f32[2,128,32]{1,0,2:T(2,128)S(1)}, u32[]{:S(2)}, u32[]{:S(2)}) async-start(f32[2,128,32]{1,0,2:T(2,128)} %copy.63), calls=%async_computation.2 | async-start | bytes 65536 | tf_op jit(solution)/shard_map/all_to_all | solution.py:101
